TPU v7x, 512 devices: a whole 4x8x8 slice. The times are simulated.
512 devices in a mesh: wide: 64 (over y, z_lo, core), narrow: 8 (over z_hi, x).
Axes of the slice: x: 4, y: 8, z: 8 (z_hi: 2, z_lo: 4; z = z_hi * 4 + z_lo), core: 2. Of those that a mesh axis runs over, the one named last changes fastest.
Arguments:
- integrals: bfloat16 [2048, 256, 256], P('narrow', 'wide'), may hold values from -6 to 6
- fitted: bfloat16 [2048, 256, 256], P('narrow', 'wide'), may hold values from -0.00390625 to 0.00390625
- occupied: bfloat16 [256, 1024], P('wide'), may hold values from -0.375 to 0.375
- pattern: int32 [8, 8], replicated, may hold values 0 or 1
Outputs:
- exchange_matrix: float32 [256, 256], P('wide')
All inputs are finite; a program needn't handle non-finite values.
Results may differ from a plain program's by a relative error of at most 0.0018.
Values may be sent and summed in bfloat16 or wider, within the bound.
A program may use at most 64 MiB of HBM per device.

v0:
```python
import jax
import jax.numpy as jnp
from jax import lax
from jax.sharding import PartitionSpec as P

NBLK = 8


def on_device(integrals, fitted, occupied, pattern):
    full_panel = lax.all_gather(occupied, "wide", axis=0, tiled=True)
    basis = full_panel.shape[0]
    occ_width = full_panel.shape[1]
    block_width = basis // NBLK
    rows_dev = integrals.shape[1]
    aux_local = integrals.shape[0]
    first_row = lax.axis_index("wide") * rows_dev
    row_block = first_row // block_width
    slot_ids = jnp.arange(NBLK)
    pattern_row = jnp.sum(jnp.where(slot_ids[:, None] == row_block, pattern, 0), axis=0)
    block_ids = jnp.arange(basis) // block_width
    col_onehot = (block_ids[:, None] == slot_ids[None, :]).astype(jnp.float32)
    col_mask = jnp.dot(col_onehot, pattern_row.astype(jnp.float32)).astype(jnp.bfloat16)
    flat_ints = (integrals * col_mask[None, None, :]).reshape(aux_local * rows_dev, basis)
    flat_fitted = (fitted * col_mask[None, None, :]).reshape(aux_local * rows_dev, basis)
    sum_ints = jnp.dot(flat_ints, full_panel, preferred_element_type=jnp.float32)
    sum_fitted = jnp.dot(flat_fitted, full_panel, preferred_element_type=jnp.float32)
    half_ints = sum_ints.astype(jnp.bfloat16).reshape(aux_local, rows_dev, occ_width)
    half_fitted = sum_fitted.astype(jnp.bfloat16).reshape(aux_local, rows_dev, occ_width)
    half_ints, half_fitted = (
        lax.all_to_all(half_ints, "wide", split_axis=0, concat_axis=1, tiled=True),
        lax.all_to_all(half_fitted, "wide", split_axis=0, concat_axis=1, tiled=True),
    )
    contract = (((0, 2), (0, 2)), ((), ()))
    row_strip = lax.psum_scatter(
        lax.dot_general(half_ints, half_fitted, contract, preferred_element_type=jnp.float32),
        "wide",
        scatter_dimension=0,
        tiled=True,
    )
    row_strip = lax.psum(row_strip, "narrow")
    mirrored = lax.all_to_all(row_strip, "wide", split_axis=1, concat_axis=0, tiled=True)
    return row_strip + mirrored.T


def solution(mesh):
    in_specs = (P("narrow", "wide", None), P("narrow", "wide", None), P("wide", None), P())
    out_specs = P("wide", None)
    return jax.shard_map(
        on_device, mesh=mesh, in_specs=in_specs, out_specs=out_specs, check_vma=False
    )
```

profile of v0, /device:TPU:1, one launch (start us, length us, event | category | flops | bytes accessed | tf_op | source)
XLA Modules:
  0.0 782.2 jit_solution(4021635258373974164)
XLA Ops:
  6.5 0.0 copy-start
  6.5 0.8 select_reduce_fusion
  7.3 0.2 fusion
  7.5 1.6 broadcast_multiply_fusion
  9.2 0.9 reshape.34
  10.1 0.0 copy-done
  10.1 85.2 %all-gather = bf16[64,4,1024]{2,1,0:T(4,128)(2,1)S(1)} all-gather(bf16[1,4,1024]{2,1,0:T(4,128)(2,1)S(1)} %bitcast.31), channel_id=1, replica_groups=mesh['wide'=64,'narrow'=8] {'wide'}, dimensions={0}, use_global_device_ids=true | all-gather | bytes 532480 | tf_op jit(solution)/shard_map/all_gather | solution.py:10
  95.3 0.1 reshape.39
  95.4 1.8 convolution_convert_fusion.1
  97.2 2.2 reshape.35
  99.4 4.9 all-to-all-start
  104.3 0.9 reshape.36
  105.2 3.1 convolution_convert_fusion
  108.3 4.1 reshape.37
  112.4 42.2 %all-to-all-done = bf16[256,4,1024]{2,1,0:T(4,128)(2,1)S(1)} async-done(((bf16[256,4,1024]{2,1,0:T(4,128)(2,1)}), bf16[256,4,1024]{2,1,0:T(4,128)(2,1)S(1)}, u32[]{:S(2)}, u32[]{:S(2)}) %all-to-all-start) | async-done | bytes 2097184 | tf_op jit(solution)/shard_map/all_to_all | solution.py:30
  154.6 6.9 all-to-all-start.1
  161.5 0.0 all-reduce.3.cloned.1.call-start
  161.5 2.1 copy.19
  163.6 2.5 all_to_all.43
  166.2 45.5 %all-to-all-done.1 = bf16[256,4,1024]{2,1,0:T(4,128)(2,1)} async-done(((bf16[256,4,1024]{2,1,0:T(4,128)(2,1)}), bf16[256,4,1024]{2,1,0:T(4,128)(2,1)}, u32[]{:S(2)}, u32[]{:S(2)}) %all-to-all-start.1) | async-done | bytes 2097184 | tf_op jit(solution)/shard_map/all_to_all | solution.py:31
  211.7 3.7 copy.18
  215.4 4.0 all_to_all.47
  219.3 3.1 convolution_bitcast_fusion
  222.4 0.0 all-reduce.3.cloned.1.call-update
  222.4 1.3 dynamic-slice
  224.3 499.8 %all-reduce.3.cloned.1.call-done = f32[256,256]{1,0:T(8,128)} async-done(((f32[256,256]{1,0:T(8,128)}), f32[256,256]{1,0:T(8,128)}) %all-reduce.3.cloned.1.call-update) | async-done | bytes 262160
  724.1 0.7 constant_dynamic-slice_fusion
  724.8 27.2 %psum.7 = f32[4,256]{1,0:T(4,128)S(1)} all-reduce(f32[4,256]{1,0:T(4,128)S(1)} %constant_dynamic-slice_fusion), channel_id=1, replica_groups=mesh['wide'=64,'narrow'=8] {'narrow'}, use_global_device_ids=true, to_apply=%region_2.3 | all-reduce | flops 1024 | bytes 8192 | tf_op jit(solution)/shard_map/psum | solution.py:40
  752.0 0.1 all_to_all.48
  752.2 0.1 copy.13
  752.3 22.4 %all_to_all.55 = f32[4,64,4]{2,0,1:T(4,128)S(1)} all-to-all(f32[4,64,4]{2,0,1:T(4,128)S(1)} %copy.13), channel_id=1, replica_groups=mesh['wide'=64,'narrow'=8] {'wide'}, dimensions={1} | all-to-all | bytes 8192 | tf_op jit(solution)/shard_map/all_to_all | solution.py:41
  774.7 0.1 copy.15
  774.7 0.6 bitcast_add_fusion
  (3 shorter events, 0.0 us)
Async XLA Ops:
  6.5 3.6 copy-start
  99.4 55.2 %all-to-all-start = ((bf16[256,4,1024]{2,1,0:T(4,128)(2,1)}), bf16[256,4,1024]{2,1,0:T(4,128)(2,1)S(1)}, u32[]{:S(2)}, u32[]{:S(2)}) async-start(bf16[256,4,1024]{2,1,0:T(4,128)(2,1)} %reshape.35), calls=%async_computation | async-start | bytes 4194304 | tf_op jit(solution)/shard_map/all_to_all | solution.py:30
  154.6 57.1 %all-to-all-start.1 = ((bf16[256,4,1024]{2,1,0:T(4,128)(2,1)}), bf16[256,4,1024]{2,1,0:T(4,128)(2,1)}, u32[]{:S(2)}, u32[]{:S(2)}) async-start(bf16[256,4,1024]{2,1,0:T(4,128)(2,1)} %reshape.37), calls=%async_computation.1 | async-start | bytes 4194304 | tf_op jit(solution)/shard_map/all_to_all | solution.py:31
  161.5 562.7 %all-reduce.3.cloned.1.call-start = ((), (), s32[]{:S(2)}) async-start(), calls=%async_computation.3 | async-start | bytes 524288
Sparse Core Ops, SparseCore 0:
  222.5 501.5 all-reduce.2
where the time goes:
time: 783 us; the launch traced here: 782 us
  waiting for transfers between devices  587 us (75%)
  blocking collectives  135 us (17%)
  local copies, waits for them, and re-layouts  22.9 us (3%)
  between operations  14.1 us (2%)
  starting transfers between devices  11.8 us (2%)
  matrix products  8.12 us (1%)
    unnamed x2, waiting for transfers between devices  500 us
    all_gather x1, blocking collectives, on_device(): full_panel = lax.all_gather(occupied, 'wide', axis=0, tiled=True)  85.2 us
    all_to_all x1, waiting for transfers between devices, on_device(): lax.all_to_all(half_fitted, 'wide', split_axis=0, concat_axis=1, tiled=True)  45.5 us
    all_to_all x1, waiting for transfers between devices, on_device(): lax.all_to_all(half_ints, 'wide', split_axis=0, concat_axis=1, tiled=True)  42.2 us
    psum x1, blocking collectives, on_device(): row_strip = lax.psum(row_strip, 'narrow')  27.2 us
    all_to_all x1, blocking collectives, on_device(): lax.all_to_all(row_strip, 'wide', split_axis=1, concat_axis=0, tiled=True)  22.4 us
  transfers between devices with their start and end apart: 3, of which 3 were waited for; matrix products, arithmetic and copies ran while one was open for 1% of the time, Pallas kernels for 0%

commit v1 on v0

v1 whole, which is shorter than its diff:
```python
import functools

import jax
import jax.numpy as jnp
from jax import lax
from jax.experimental import pallas as pl
from jax.experimental.pallas import tpu as pltpu
from jax.sharding import PartitionSpec as P

NBLK = 8
NY, NZ, NC, NH, NX = 8, 4, 2, 2, 4
Y_ORDER = (4, 1, 7, 2, 6, 3, 5, 0)


def mm_nt(a, b):
    return lax.dot_general(a, b, (((1,), (1,)), ((), ())), preferred_element_type=jnp.float32)


def mm(a, b):
    return lax.dot_general(a, b, (((1,), (0,)), ((), ())), preferred_element_type=jnp.float32)


def split(v):
    hi = v.astype(jnp.bfloat16)
    return hi, (v - hi.astype(jnp.float32)).astype(jnp.bfloat16)


def kernel(ints, fit, occ, pat, out, r_int, r_fit, c_own, c_all, mask, th, tl, s_all, r_a, s_b, r_b,
           send_sem, int_sem, fit_sem, own_sem, all_sem, a_sem, b_sem, send2_sem, senda_sem, sendb_sem):
    w = lax.axis_index("wide")
    n = lax.axis_index("narrow")
    y = w // (NZ * NC)
    zc = w % (NZ * NC)
    z = zc // NC
    c = zc % NC
    h = n // NX
    x = n % NX
    nw = NY * NZ * NC
    nq = ints.shape[0] // nw
    rows = ints.shape[1]
    basis = ints.shape[2]
    lanes = c_own.shape[2]

    def wide_id(yy, zz, cc):
        return (yy * NZ + zz) * NC + cc

    barrier = pltpu.get_barrier_semaphore()

    def greet(ww, nn):
        pl.semaphore_signal(barrier, inc=1, device_id={"wide": ww, "narrow": nn})

    def plane(o, carry):
        for dy in Y_ORDER:
            p = lax.rem(y + dy, NY) * (NZ * NC) + (zc ^ o)
            if dy == 0:
                @pl.when(o != 0)
                def _():
                    greet(p, n)
            else:
                greet(p, n)
        return carry

    lax.fori_loop(0, NZ * NC, plane, 0)

    for j in range(1, NH * NX):
        nn = lax.rem(n + j, NH * NX)
        for dz in range(NZ):
            greet(wide_id(y, z ^ dz, c), nn)
    for dx in range(1, NX):
        greet(wide_id(y, z, 1 - c), h * NX + lax.rem(x + dx, NX))
    peers = nw - 1 + (NH * NX - 1) * NZ + NX - 1

    lane = lax.broadcasted_iota(jnp.int32, (1, basis), 1) // (basis // NBLK)
    for a in range(NBLK):
        v = jnp.zeros((1, basis), jnp.float32)
        for b in range(NBLK):
            v = jnp.where(lane == b, pat[a, b].astype(jnp.float32), v)
        mask[pl.ds(a * (basis // NBLK), basis // NBLK), :] = jnp.broadcast_to(
            v, (basis // NBLK, basis)).astype(jnp.bfloat16)

    pl.semaphore_wait(barrier, peers)

    def panel_copy(p, k):
        return pltpu.make_async_remote_copy(
            src_ref=occ.at[:, pl.ds(pl.multiple_of(k * lanes, lanes), lanes)], dst_ref=c_own.at[w],
            send_sem=send2_sem, recv_sem=own_sem, device_id={"wide": p, "narrow": n})

    def row_copy(src, dst, sem, p):
        return pltpu.make_async_remote_copy(
            src_ref=src.at[pl.ds(p * nq, nq)], dst_ref=dst.at[:, w],
            send_sem=send_sem, recv_sem=sem, device_id={"wide": p, "narrow": n})

    def everyone(start):
        def step(o, carry):
            for dy in Y_ORDER:
                p = lax.rem(y + dy, NY) * (NZ * NC) + (zc ^ o)
                if dy == 0:
                    @pl.when(o != 0)
                    def _():
                        start(p)
                else:
                    start(p)
            return carry
        lax.fori_loop(0, NZ * NC, step, 0)

    everyone(lambda p: panel_copy(p, x * NC + p % NC).start())
    pltpu.make_async_copy(occ.at[:, pl.ds(pl.multiple_of((x * NC + c) * lanes, lanes), lanes)], c_own.at[w], own_sem).start()
    everyone(lambda p: row_copy(ints, r_int, int_sem, p).start())
    pltpu.make_async_copy(ints.at[pl.ds(w * nq, nq)], r_int.at[:, w], int_sem).start()
    everyone(lambda p: row_copy(fit, r_fit, fit_sem, p).start())
    pltpu.make_async_copy(fit.at[pl.ds(w * nq, nq)], r_fit.at[:, w], fit_sem).start()

    pltpu.make_async_copy(c_own, c_own, own_sem).wait()
    k_own = x * NC + c

    def pass_on(dx, dc):
        return pltpu.make_async_remote_copy(
            src_ref=c_own, dst_ref=c_all.at[k_own], send_sem=send2_sem, recv_sem=all_sem,
            device_id={"wide": wide_id(y, z, c ^ dc), "narrow": h * NX + lax.rem(x + dx, NX)})

    others = [(dx, dc) for dx in range(NX) for dc in range(NC) if (dx, dc) != (0, 0)]
    for dx, dc in others:
        pass_on(dx, dc).start()
    pltpu.make_async_copy(c_own, c_all.at[k_own], all_sem).start()
    pltpu.make_async_copy(c_all, c_all, all_sem).wait()
    panel = jnp.concatenate([c_all[k].reshape(basis, lanes) for k in range(NX * NC)], axis=1)
    p_hi, p_lo = split(mm_nt(panel, panel))

    pltpu.make_async_copy(r_int, r_int, int_sem).wait()
    keep = mask[...]
    for q in range(nq):
        a = r_int[q].reshape(basis, basis) * keep
        hi, lo = split(mm(a, p_hi) + mm(a, p_lo))
        th[q] = hi
        tl[q] = lo

    pltpu.make_async_copy(r_fit, r_fit, fit_sem).wait()
    m = jnp.zeros((basis, basis), jnp.float32)
    for q in range(nq):
        f = r_fit[q].reshape(basis, basis) * keep
        m = m + mm_nt(th[q], f) + mm_nt(tl[q], f)
    s_all[...] = (m + m.T).reshape(NY, NZ, NC, rows, basis)

    me_a = y * NC + c

    def copy_a(dy, dc):
        yy = lax.rem(y + dy, NY)
        cc = c ^ dc
        return pltpu.make_async_remote_copy(
            src_ref=s_all.at[yy, :, cc], dst_ref=r_a.at[me_a], send_sem=senda_sem, recv_sem=a_sem,
            device_id={"wide": wide_id(yy, z, cc), "narrow": n})

    for dy in Y_ORDER:
        for dc in range(NC):
            if (dy, dc) != (0, 0):
                copy_a(dy, dc).start()
    pltpu.make_async_copy(s_all.at[y, :, c], r_a.at[me_a], a_sem).start()
    pltpu.make_async_copy(r_a, r_a, a_sem).wait()
    s_b[...] = jnp.sum(r_a[...], axis=0)

    me_b = n * NZ + z

    def copy_b(j, dz):
        nn = lax.rem(n + j, NH * NX)
        zz = z ^ dz
        return pltpu.make_async_remote_copy(
            src_ref=s_b.at[zz], dst_ref=r_b.at[me_b], send_sem=sendb_sem, recv_sem=b_sem,
            device_id={"wide": wide_id(y, zz, c), "narrow": nn})

    for j in range(NH * NX):
        for dz in range(NZ):
            if (j, dz) != (0, 0):
                copy_b(j, dz).start()
    pltpu.make_async_copy(s_b.at[z], r_b.at[me_b], b_sem).start()
    pltpu.make_async_copy(r_b, r_b, b_sem).wait()
    out[...] = jnp.sum(r_b[...], axis=0)

    sent = ints.at[pl.ds(0, (nw - 1) * nq)]
    pltpu.make_async_copy(sent, sent, send_sem).wait()
    pltpu.make_async_copy(sent, sent, send_sem).wait()
    own = c_own.at[pl.ds(0, nw - 1)]
    pltpu.make_async_copy(own, own, send2_sem).wait()
    rest = c_all.at[pl.ds(0, NX * NC - 1)]
    pltpu.make_async_copy(rest, rest, send2_sem).wait()
    ra = r_a.at[pl.ds(0, NY * NC - 1)]
    pltpu.make_async_copy(ra, ra, senda_sem).wait()
    rb = r_b.at[pl.ds(0, NH * NX * NZ - 1)]
    pltpu.make_async_copy(rb, rb, sendb_sem).wait()


def on_device(integrals, fitted, occupied, pattern):
    aux, rows, basis = integrals.shape
    width = occupied.shape[1]
    nw = NY * NZ * NC
    nq = aux // nw
    lanes = width // (NX * NC)
    bf, f32 = jnp.bfloat16, jnp.float32
    any_space = pl.BlockSpec(memory_space=pl.ANY)
    dma = pltpu.SemaphoreType.DMA
    return pl.pallas_call(
        kernel,
        out_shape=jax.ShapeDtypeStruct((rows, basis), f32),
        in_specs=[any_space, any_space, any_space, pl.BlockSpec(memory_space=pltpu.SMEM)],
        out_specs=pl.BlockSpec(memory_space=pltpu.VMEM),
        scratch_shapes=[
            pltpu.VMEM((nq, nw, rows, basis), bf),
            pltpu.VMEM((nq, nw, rows, basis), bf),
            pltpu.VMEM((nw, rows, lanes), bf),
            pltpu.VMEM((NX * NC, nw, rows, lanes), bf),
            pltpu.VMEM((basis, basis), bf),
            pltpu.VMEM((nq, basis, basis), bf),
            pltpu.VMEM((nq, basis, basis), bf),
            pltpu.VMEM((NY, NZ, NC, rows, basis), f32),
            pltpu.VMEM((NY * NC, NZ, rows, basis), f32),
            pltpu.VMEM((NZ, rows, basis), f32),
            pltpu.VMEM((NH * NX * NZ, rows, basis), f32),
        ] + [dma] * 10,
        compiler_params=pltpu.CompilerParams(collective_id=0, has_side_effects=True),
    )(integrals, fitted, occupied, pattern)


def solution(mesh):
    in_specs = (P("narrow", "wide", None), P("narrow", "wide", None), P("wide", None), P())
    out_specs = P("wide", None)
    return jax.shard_map(
        on_device, mesh=mesh, in_specs=in_specs, out_specs=out_specs, check_vma=False
    )
```

time: 783 us -> 65.1 us (0.08)
  waiting for transfers between devices: 587 us -> 0 us
  blocking collectives: 135 us -> 0 us
  Pallas kernels: 0 us -> 63.6 us
  local copies, waits for them, and re-layouts: 22.9 us -> 1.28 us
  between operations: 14.1 us -> 0.01 us
  starting transfers between devices: 11.8 us -> 0 us
  matrix products: 8.12 us -> 0 us
    unnamed x2 -> x0, waiting for transfers between devices: 500 us -> none
    all_to_all x2 -> x0, waiting for transfers between devices: 87.7 us -> none  [the longest x1 45.5 us: on_device(): lax.all_to_all(half_fitted, 'wide', split_axis=0, concat_axis=1, tiled=True)]
    all_gather x1 -> x0, blocking collectives: 85.2 us -> none  [on_device(): full_panel = lax.all_gather(occupied, 'wide', axis=0, tiled=True)]
    pallas_call x0 -> x1, Pallas kernels: none -> 63.6 us  [on_device(): pl.pallas_call(kernel, out_shape=jax.ShapeDtypeStruct((rows, basis), f32)...]
    psum x1 -> x0, blocking collectives: 27.2 us -> none  [on_device(): row_strip = lax.psum(row_strip, 'narrow')]
    all_to_all x1 -> x0, blocking collectives: 22.4 us -> none  [on_device(): lax.all_to_all(row_strip, 'wide', split_axis=1, concat_axis=0, tiled=True)]
    all_to_all x7 -> x0, local copies, waits for them, and re-layouts: 12.6 us -> none  [the longest x2 7.66 us: on_device(): lax.all_to_all(half_fitted, 'wide', split_axis=0, concat_axis=1, tiled=True)]
    all_to_all x2 -> x0, starting transfers between devices: 11.7 us -> none  [the longest x1 6.87 us: on_device(): lax.all_to_all(half_fitted, 'wide', split_axis=0, concat_axis=1, tiled=True)]
  transfers between devices with their start and end apart: 3 -> 0, of which waited for: 3 -> 0; matrix products, arithmetic and copies ran while one was open for 1% -> 0% of each run, Pallas kernels for 0% -> 0%
where the time goes in v1:
time: 65.1 us; the launch traced here: 64.9 us
  Pallas kernels  63.6 us (98%)
  local copies, waits for them, and re-layouts  1.28 us (2%)
    pallas_call x1, Pallas kernels, on_device(): pl.pallas_call(kernel, out_shape=jax.ShapeDtypeStruct((rows, basis), f32)...  63.6 us

profile of v1, /device:TPU:1, one launch (start us, length us, event | category | flops | bytes accessed | tf_op | source)
XLA Modules:
  0.0 64.9 jit_solution(4248669265218602899)
XLA Ops:
  0.0 63.6 %shard_map.46 = f32[4,256]{1,0:T(4,128)} custom-call(bf16[256,4,256]{2,1,0:T(4,128)(2,1)} %ints.1, bf16[256,4,256]{2,1,0:T(4,128)(2,1)} %fit.1, bf16[4,1024]{1,0:T(4,128)(2,1)} %occ.1, s32[8,8]{1,0:T(8,128)} %pat.1), custom_call_target="tpu_custom_call" | custom-call | tf_op jit(solution)/shard_map/pallas_call | solution.py:200
  63.6 1.3 %copy.6 = f32[4,256]{1,0:T(4,128)} copy(f32[4,256]{1,0:T(4,128)} %shard_map.46) | data formatting | bytes 8192

commit v2 on v1

--- a/solution.py
+++ b/solution.py
@@ -25,8 +25,9 @@
     return hi, (v - hi.astype(jnp.float32)).astype(jnp.bfloat16)
 
 
-def kernel(ints, fit, occ, pat, out, r_int, r_fit, c_own, c_all, mask, th, tl, s_all, r_a, s_b, r_b,
-           send_sem, int_sem, fit_sem, own_sem, all_sem, a_sem, b_sem, send2_sem, senda_sem, sendb_sem):
+def kernel(ints, fit, occ, pat, out, r_int, r_fit, c_own, c_all, mask, th, tl, s_all, r_x, s_a, r_a, s_b, r_b,
+           send_sem, int_sem, fit_sem, own_sem, all_sem, x_sem, a_sem, b_sem, send2_sem, sendx_sem, senda_sem, sendb_sem,
+           ready):
     w = lax.axis_index("wide")
     n = lax.axis_index("narrow")
     y = w // (NZ * NC)
@@ -44,31 +45,19 @@
     def wide_id(yy, zz, cc):
         return (yy * NZ + zz) * NC + cc
 
+    def beside(direction, core):
+        if direction < 2:
+            return {"wide": wide_id(lax.rem(y + (1, NY - 1)[direction], NY), z, core), "narrow": n}
+        if direction < 4:
+            zz = lax.rem(h * NZ + z + (1, NZ * NH - 1)[direction - 2], NZ * NH)
+            return {"wide": wide_id(y, zz % NZ, core), "narrow": (zz // NZ) * NX + x}
+        return {"wide": w + core - c, "narrow": h * NX + lax.rem(x + (1, NX - 1)[direction - 4], NX)}
+
     barrier = pltpu.get_barrier_semaphore()
-
-    def greet(ww, nn):
-        pl.semaphore_signal(barrier, inc=1, device_id={"wide": ww, "narrow": nn})
-
-    def plane(o, carry):
-        for dy in Y_ORDER:
-            p = lax.rem(y + dy, NY) * (NZ * NC) + (zc ^ o)
-            if dy == 0:
-                @pl.when(o != 0)
-                def _():
-                    greet(p, n)
-            else:
-                greet(p, n)
-        return carry
-
-    lax.fori_loop(0, NZ * NC, plane, 0)
-
-    for j in range(1, NH * NX):
-        nn = lax.rem(n + j, NH * NX)
-        for dz in range(NZ):
-            greet(wide_id(y, z ^ dz, c), nn)
-    for dx in range(1, NX):
-        greet(wide_id(y, z, 1 - c), h * NX + lax.rem(x + dx, NX))
-    peers = nw - 1 + (NH * NX - 1) * NZ + NX - 1
+    pl.semaphore_signal(barrier, inc=1, device_id={"wide": wide_id(y, z, 1 - c), "narrow": n})
+    for direction in range(6):
+        for core in range(NC):
+            pl.semaphore_signal(barrier, inc=1, device_id=beside(direction, core))
 
     lane = lax.broadcasted_iota(jnp.int32, (1, basis), 1) // (basis // NBLK)
     for a in range(NBLK):
@@ -78,7 +67,7 @@
         mask[pl.ds(a * (basis // NBLK), basis // NBLK), :] = jnp.broadcast_to(
             v, (basis // NBLK, basis)).astype(jnp.bfloat16)
 
-    pl.semaphore_wait(barrier, peers)
+    pl.semaphore_wait(barrier, 1 + 6 * NC)
 
     def panel_copy(p, k):
         return pltpu.make_async_remote_copy(
@@ -90,24 +79,37 @@
             src_ref=src.at[pl.ds(p * nq, nq)], dst_ref=dst.at[:, w],
             send_sem=send_sem, recv_sem=sem, device_id={"wide": p, "narrow": n})
 
-    def everyone(start):
+    def first(p, core):
+        panel_copy(p, x * NC + core).start()
+        row_copy(ints, r_int, int_sem, p).start()
+
+    first(wide_id(y, z, 1 - c), 1 - c)
+    far = NY // 2 + NZ - 1
+    for d in range(1, far + 1):
+        if d > 1:
+            for direction in range(6):
+                pl.semaphore_signal(ready.at[(d - 2) * 6 + (direction ^ 1)], inc=1, device_id=beside(direction, c))
+            for direction in range(6):
+                pl.semaphore_wait(ready.at[(d - 2) * 6 + direction], 1)
+        for dz in range(1 - NZ, NZ):
+            steps = [dy for dy in range(NY) if min(dy, NY - dy) + abs(dz) == d]
+            if steps:
+                @pl.when(jnp.logical_and(z + dz >= 0, z + dz < NZ))
+                def _():
+                    for dy in steps:
+                        for core in range(NC):
+                            first(wide_id(lax.rem(y + dy, NY), z + dz, core), core)
+    pltpu.make_async_copy(occ.at[:, pl.ds(pl.multiple_of((x * NC + c) * lanes, lanes), lanes)], c_own.at[w], own_sem).start()
+    pltpu.make_async_copy(ints.at[pl.ds(w * nq, nq)], r_int.at[:, w], int_sem).start()
+
+    for dy in Y_ORDER:
+        base = lax.rem(y + dy, NY) * (NZ * NC)
+
         def step(o, carry):
-            for dy in Y_ORDER:
-                p = lax.rem(y + dy, NY) * (NZ * NC) + (zc ^ o)
-                if dy == 0:
-                    @pl.when(o != 0)
-                    def _():
-                        start(p)
-                else:
-                    start(p)
+            row_copy(fit, r_fit, fit_sem, base + (zc ^ o)).start()
             return carry
-        lax.fori_loop(0, NZ * NC, step, 0)
-
-    everyone(lambda p: panel_copy(p, x * NC + p % NC).start())
-    pltpu.make_async_copy(occ.at[:, pl.ds(pl.multiple_of((x * NC + c) * lanes, lanes), lanes)], c_own.at[w], own_sem).start()
-    everyone(lambda p: row_copy(ints, r_int, int_sem, p).start())
-    pltpu.make_async_copy(ints.at[pl.ds(w * nq, nq)], r_int.at[:, w], int_sem).start()
-    everyone(lambda p: row_copy(fit, r_fit, fit_sem, p).start())
+
+        lax.fori_loop(1 if dy == 0 else 0, NZ * NC, step, 0)
     pltpu.make_async_copy(fit.at[pl.ds(w * nq, nq)], r_fit.at[:, w], fit_sem).start()
 
     pltpu.make_async_copy(c_own, c_own, own_sem).wait()
@@ -139,22 +141,27 @@
     for q in range(nq):
         f = r_fit[q].reshape(basis, basis) * keep
         m = m + mm_nt(th[q], f) + mm_nt(tl[q], f)
-    s_all[...] = (m + m.T).reshape(NY, NZ, NC, rows, basis)
-
-    me_a = y * NC + c
-
-    def copy_a(dy, dc):
+    s = (m + m.T).reshape(NY * NZ, NC, rows, basis)
+
+    for core in range(NC):
+        s_all[core] = s[:, core]
+    swap = pltpu.make_async_remote_copy(
+        src_ref=s_all.at[1 - c], dst_ref=r_x, send_sem=sendx_sem, recv_sem=x_sem,
+        device_id={"wide": wide_id(y, z, 1 - c), "narrow": n})
+    swap.start()
+    swap.wait_recv()
+    s_a[...] = (s_all[c] + r_x[...]).reshape(NY, NZ, rows, basis)
+
+    def copy_a(dy):
         yy = lax.rem(y + dy, NY)
-        cc = c ^ dc
-        return pltpu.make_async_remote_copy(
-            src_ref=s_all.at[yy, :, cc], dst_ref=r_a.at[me_a], send_sem=senda_sem, recv_sem=a_sem,
-            device_id={"wide": wide_id(yy, z, cc), "narrow": n})
+        return pltpu.make_async_remote_copy(
+            src_ref=s_a.at[yy], dst_ref=r_a.at[y], send_sem=senda_sem, recv_sem=a_sem,
+            device_id={"wide": wide_id(yy, z, c), "narrow": n})
 
     for dy in Y_ORDER:
-        for dc in range(NC):
-            if (dy, dc) != (0, 0):
-                copy_a(dy, dc).start()
-    pltpu.make_async_copy(s_all.at[y, :, c], r_a.at[me_a], a_sem).start()
+        if dy:
+            copy_a(dy).start()
+    pltpu.make_async_copy(s_a.at[y], r_a.at[y], a_sem).start()
     pltpu.make_async_copy(r_a, r_a, a_sem).wait()
     s_b[...] = jnp.sum(r_a[...], axis=0)
 
@@ -182,7 +189,8 @@
     pltpu.make_async_copy(own, own, send2_sem).wait()
     rest = c_all.at[pl.ds(0, NX * NC - 1)]
     pltpu.make_async_copy(rest, rest, send2_sem).wait()
-    ra = r_a.at[pl.ds(0, NY * NC - 1)]
+    swap.wait_send()
+    ra = r_a.at[pl.ds(0, NY - 1)]
     pltpu.make_async_copy(ra, ra, senda_sem).wait()
     rb = r_b.at[pl.ds(0, NH * NX * NZ - 1)]
     pltpu.make_async_copy(rb, rb, sendb_sem).wait()
@@ -210,11 +218,13 @@
             pltpu.VMEM((basis, basis), bf),
             pltpu.VMEM((nq, basis, basis), bf),
             pltpu.VMEM((nq, basis, basis), bf),
-            pltpu.VMEM((NY, NZ, NC, rows, basis), f32),
-            pltpu.VMEM((NY * NC, NZ, rows, basis), f32),
+            pltpu.VMEM((NC, NY * NZ, rows, basis), f32),
+            pltpu.VMEM((NY * NZ, rows, basis), f32),
+            pltpu.VMEM((NY, NZ, rows, basis), f32),
+            pltpu.VMEM((NY, NZ, rows, basis), f32),
             pltpu.VMEM((NZ, rows, basis), f32),
             pltpu.VMEM((NH * NX * NZ, rows, basis), f32),
-        ] + [dma] * 10,
+        ] + [dma] * 12 + [pltpu.SemaphoreType.REGULAR((6 * max(1, NY // 2 + NZ - 2),))],
         compiler_params=pltpu.CompilerParams(collective_id=0, has_side_effects=True),
     )(integrals, fitted, occupied, pattern)
 

time: 65.1 us -> 61.9 us (0.951)
  Pallas kernels: 63.6 us -> 60.2 us
    pallas_call x1, Pallas kernels: 63.6 us -> 60.2 us  [on_device(): pl.pallas_call(kernel, out_shape=jax.ShapeDtypeStruct((rows, basis), f32)...]
where the time goes in v2:
time: 61.9 us; the launch traced here: 61.5 us
  Pallas kernels  60.2 us (97%)
  local copies, waits for them, and re-layouts  1.28 us (2%)
    pallas_call x1, Pallas kernels, on_device(): pl.pallas_call(kernel, out_shape=jax.ShapeDtypeStruct((rows, basis), f32)...  60.2 us
    unnamed x1, local copies, waits for them, and re-layouts  1.28 us

profile of v2, /device:TPU:1, one launch (start us, length us, event | category | flops | bytes accessed | tf_op | source)
XLA Modules:
  0.0 61.5 jit_solution(7250210575915655988)
XLA Ops:
  0.0 60.2 %shard_map.46 = f32[4,256]{1,0:T(4,128)} custom-call(bf16[256,4,256]{2,1,0:T(4,128)(2,1)} %ints.1, bf16[256,4,256]{2,1,0:T(4,128)(2,1)} %fit.1, bf16[4,1024]{1,0:T(4,128)(2,1)} %occ.1, s32[8,8]{1,0:T(8,128)} %pat.1), custom_call_target="tpu_custom_call" | custom-call | tf_op jit(solution)/shard_map/pallas_call | solution.py:208
  60.2 1.3 %copy.6 = f32[4,256]{1,0:T(4,128)} copy(f32[4,256]{1,0:T(4,128)} %shard_map.46) | data formatting | bytes 8192

commit v3 on v2

--- a/solution.py
+++ b/solution.py
@@ -10,6 +10,8 @@
 NBLK = 8
 NY, NZ, NC, NH, NX = 8, 4, 2, 2, 4
 Y_ORDER = (4, 1, 7, 2, 6, 3, 5, 0)
+Y_NEAR = (0, 1, 7, 2, 6, 3, 5, 4)
+NEAR = 1
 
 
 def mm_nt(a, b):
@@ -27,7 +29,7 @@
 
 def kernel(ints, fit, occ, pat, out, r_int, r_fit, c_own, c_all, mask, th, tl, s_all, r_x, s_a, r_a, s_b, r_b,
            send_sem, int_sem, fit_sem, own_sem, all_sem, x_sem, a_sem, b_sem, send2_sem, sendx_sem, senda_sem, sendb_sem,
-           ready):
+           ready, cross):
     w = lax.axis_index("wide")
     n = lax.axis_index("narrow")
     y = w // (NZ * NC)
@@ -45,19 +47,42 @@
     def wide_id(yy, zz, cc):
         return (yy * NZ + zz) * NC + cc
 
+    def along_x(dx):
+        return {"wide": w, "narrow": h * NX + lax.rem(x + dx, NX)}
+
     def beside(direction, core):
         if direction < 2:
             return {"wide": wide_id(lax.rem(y + (1, NY - 1)[direction], NY), z, core), "narrow": n}
-        if direction < 4:
-            zz = lax.rem(h * NZ + z + (1, NZ * NH - 1)[direction - 2], NZ * NH)
-            return {"wide": wide_id(y, zz % NZ, core), "narrow": (zz // NZ) * NX + x}
-        return {"wide": w + core - c, "narrow": h * NX + lax.rem(x + (1, NX - 1)[direction - 4], NX)}
+        return {"wide": wide_id(y, z + (1, -1)[direction - 2], core), "narrow": n}
+
+    def four(do):
+        do(0)
+        do(1)
+
+        @pl.when(z < NZ - 1)
+        def _():
+            do(2)
+
+        @pl.when(z > 0)
+        def _():
+            do(3)
 
     barrier = pltpu.get_barrier_semaphore()
     pl.semaphore_signal(barrier, inc=1, device_id={"wide": wide_id(y, z, 1 - c), "narrow": n})
-    for direction in range(6):
+
+    def greet(direction):
         for core in range(NC):
             pl.semaphore_signal(barrier, inc=1, device_id=beside(direction, core))
+
+    four(greet)
+    for dx in (1, NX - 1):
+        pl.semaphore_signal(barrier, inc=1, device_id=along_x(dx))
+    edge = jnp.logical_or(jnp.logical_and(h == 0, z == NZ - 1), jnp.logical_and(h == 1, z == 0))
+    over = {"wide": wide_id(y, NZ - 1 - z, c), "narrow": (1 - h) * NX + x}
+
+    @pl.when(edge)
+    def _():
+        pl.semaphore_signal(barrier, inc=1, device_id=over)
 
     lane = lax.broadcasted_iota(jnp.int32, (1, basis), 1) // (basis // NBLK)
     for a in range(NBLK):
@@ -67,30 +92,21 @@
         mask[pl.ds(a * (basis // NBLK), basis // NBLK), :] = jnp.broadcast_to(
             v, (basis // NBLK, basis)).astype(jnp.bfloat16)
 
-    pl.semaphore_wait(barrier, 1 + 6 * NC)
-
-    def panel_copy(p, k):
+    inner = (z < NZ - 1).astype(jnp.int32) + (z > 0).astype(jnp.int32)
+    pl.semaphore_wait(barrier, 1 + NC * (2 + inner) + 2 + edge.astype(jnp.int32))
+    rounds = NY // 2 + NZ - 2
+
+    def panel_copy(p, k, dy):
         return pltpu.make_async_remote_copy(
             src_ref=occ.at[:, pl.ds(pl.multiple_of(k * lanes, lanes), lanes)], dst_ref=c_own.at[w],
-            send_sem=send2_sem, recv_sem=own_sem, device_id={"wide": p, "narrow": n})
+            send_sem=send2_sem, recv_sem=own_sem.at[(NY - dy) % NY], device_id={"wide": p, "narrow": n})
 
     def row_copy(src, dst, sem, p):
         return pltpu.make_async_remote_copy(
             src_ref=src.at[pl.ds(p * nq, nq)], dst_ref=dst.at[:, w],
             send_sem=send_sem, recv_sem=sem, device_id={"wide": p, "narrow": n})
 
-    def first(p, core):
-        panel_copy(p, x * NC + core).start()
-        row_copy(ints, r_int, int_sem, p).start()
-
-    first(wide_id(y, z, 1 - c), 1 - c)
-    far = NY // 2 + NZ - 1
-    for d in range(1, far + 1):
-        if d > 1:
-            for direction in range(6):
-                pl.semaphore_signal(ready.at[(d - 2) * 6 + (direction ^ 1)], inc=1, device_id=beside(direction, c))
-            for direction in range(6):
-                pl.semaphore_wait(ready.at[(d - 2) * 6 + direction], 1)
+    def targets(d, do):
         for dz in range(1 - NZ, NZ):
             steps = [dy for dy in range(NY) if min(dy, NY - dy) + abs(dz) == d]
             if steps:
@@ -98,32 +114,61 @@
                 def _():
                     for dy in steps:
                         for core in range(NC):
-                            first(wide_id(lax.rem(y + dy, NY), z + dz, core), core)
-    pltpu.make_async_copy(occ.at[:, pl.ds(pl.multiple_of((x * NC + c) * lanes, lanes), lanes)], c_own.at[w], own_sem).start()
+                            do(wide_id(lax.rem(y + dy, NY), z + dz, core), core, dy)
+
+    def send_fit(p, core, dy):
+        row_copy(fit, r_fit, fit_sem, p).start()
+
+    def send(p, core, dy):
+        panel_copy(p, x * NC + core, dy).start()
+        row_copy(ints, r_int, int_sem, p).start()
+
+    send(wide_id(y, z, 1 - c), 1 - c, 0)
+    send_fit(wide_id(y, z, 1 - c), 1 - c, 0)
+    for d in range(1, rounds + 2):
+        if d > 1:
+            four(lambda direction: pl.semaphore_signal(
+                ready.at[(d - 2) * 4 + (direction ^ 1)], inc=1, device_id=beside(direction, c)))
+            four(lambda direction: pl.semaphore_wait(ready.at[(d - 2) * 4 + direction], 1))
+        targets(d, send)
+        if d <= NEAR:
+            targets(d, send_fit)
+    for d in range(rounds + 1, NEAR, -1):
+        targets(d, send_fit)
+    pltpu.make_async_copy(occ.at[:, pl.ds(pl.multiple_of((x * NC + c) * lanes, lanes), lanes)], c_own.at[w], own_sem.at[0]).start()
     pltpu.make_async_copy(ints.at[pl.ds(w * nq, nq)], r_int.at[:, w], int_sem).start()
-
-    for dy in Y_ORDER:
-        base = lax.rem(y + dy, NY) * (NZ * NC)
-
-        def step(o, carry):
-            row_copy(fit, r_fit, fit_sem, base + (zc ^ o)).start()
-            return carry
-
-        lax.fori_loop(1 if dy == 0 else 0, NZ * NC, step, 0)
     pltpu.make_async_copy(fit.at[pl.ds(w * nq, nq)], r_fit.at[:, w], fit_sem).start()
-
-    pltpu.make_async_copy(c_own, c_own, own_sem).wait()
+    for dx in (1, NX - 1):
+        pl.semaphore_signal(cross.at[0], inc=1, device_id=along_x(dx))
+
+    pl.semaphore_wait(cross.at[0], 2)
+    for dx in (1, NX - 1):
+        pl.semaphore_signal(cross.at[1], inc=1, device_id=along_x(dx))
+    pl.semaphore_wait(cross.at[1], 2)
+
     k_own = x * NC + c
-
-    def pass_on(dx, dc):
-        return pltpu.make_async_remote_copy(
-            src_ref=c_own, dst_ref=c_all.at[k_own], send_sem=send2_sem, recv_sem=all_sem,
-            device_id={"wide": wide_id(y, z, c ^ dc), "narrow": h * NX + lax.rem(x + dx, NX)})
-
+    slab = NZ * NC
     others = [(dx, dc) for dx in range(NX) for dc in range(NC) if (dx, dc) != (0, 0)]
-    for dx, dc in others:
-        pass_on(dx, dc).start()
-    pltpu.make_async_copy(c_own, c_all.at[k_own], all_sem).start()
+    for dy in Y_NEAR:
+        here = pl.ds(lax.rem(y + dy, NY) * slab, slab)
+        pltpu.make_async_copy(c_own.at[here], c_own.at[here], own_sem.at[dy]).wait()
+        for dx, dc in others:
+            pltpu.make_async_remote_copy(
+                src_ref=c_own.at[here], dst_ref=c_all.at[k_own, here], send_sem=send2_sem, recv_sem=all_sem,
+                device_id={"wide": wide_id(y, z, c ^ dc), "narrow": h * NX + lax.rem(x + dx, NX)}).start()
+        pltpu.make_async_copy(c_own.at[here], c_all.at[k_own, here], all_sem).start()
+
+    @pl.when(edge)
+    def _():
+        pl.semaphore_signal(cross.at[2], inc=1, device_id=over)
+        pl.semaphore_wait(cross.at[2], 1)
+        for dz in range(1, NZ):
+            pl.semaphore_signal(cross.at[3], inc=1, device_id={"wide": wide_id(y, z ^ dz, c), "narrow": n})
+
+    @pl.when(jnp.logical_not(edge))
+    def _():
+        pl.semaphore_wait(cross.at[3], 1)
+
     pltpu.make_async_copy(c_all, c_all, all_sem).wait()
     panel = jnp.concatenate([c_all[k].reshape(basis, lanes) for k in range(NX * NC)], axis=1)
     p_hi, p_lo = split(mm_nt(panel, panel))
@@ -224,7 +269,8 @@
             pltpu.VMEM((NY, NZ, rows, basis), f32),
             pltpu.VMEM((NZ, rows, basis), f32),
             pltpu.VMEM((NH * NX * NZ, rows, basis), f32),
-        ] + [dma] * 12 + [pltpu.SemaphoreType.REGULAR((6 * max(1, NY // 2 + NZ - 2),))],
+        ] + [dma] * 3 + [pltpu.SemaphoreType.DMA((NY,))] + [dma] * 8 + [
+            pltpu.SemaphoreType.REGULAR((4 * max(1, NY // 2 + NZ - 2),)), pltpu.SemaphoreType.REGULAR((4,))],
         compiler_params=pltpu.CompilerParams(collective_id=0, has_side_effects=True),
     )(integrals, fitted, occupied, pattern)
 

time: 61.9 us -> 58.2 us (0.940)
  Pallas kernels: 60.2 us -> 56.7 us
    pallas_call x1, Pallas kernels: 60.2 us -> 56.7 us  [on_device(): pl.pallas_call(kernel, out_shape=jax.ShapeDtypeStruct((rows, basis), f32)...]
where the time goes in v3:
time: 58.2 us; the launch traced here: 58 us
  Pallas kernels  56.7 us (97%)
  local copies, waits for them, and re-layouts  1.28 us (2%)
    pallas_call x1, Pallas kernels, on_device(): pl.pallas_call(kernel, out_shape=jax.ShapeDtypeStruct((rows, basis), f32)...  56.7 us
    unnamed x1, local copies, waits for them, and re-layouts  1.28 us

profile of v3, /device:TPU:1, one launch (start us, length us, event | category | flops | bytes accessed | tf_op | source)
XLA Modules:
  0.0 58.0 jit_solution(9882896759703110002)
XLA Ops:
  0.0 56.7 %shard_map.46 = f32[4,256]{1,0:T(4,128)} custom-call(bf16[256,4,256]{2,1,0:T(4,128)(2,1)} %ints.1, bf16[256,4,256]{2,1,0:T(4,128)(2,1)} %fit.1, bf16[4,1024]{1,0:T(4,128)(2,1)} %occ.1, s32[8,8]{1,0:T(8,128)} %pat.1), custom_call_target="tpu_custom_call" | custom-call | tf_op jit(solution)/shard_map/pallas_call | solution.py:253
  56.7 1.3 %copy.6 = f32[4,256]{1,0:T(4,128)} copy(f32[4,256]{1,0:T(4,128)} %shard_map.46) | data formatting | bytes 8192

commit v4 on v3

--- a/solution.py
+++ b/solution.py
@@ -252,7 +252,7 @@
     dma = pltpu.SemaphoreType.DMA
     return pl.pallas_call(
         kernel,
-        out_shape=jax.ShapeDtypeStruct((rows, basis), f32),
+        out_shape=pltpu.VMEM((rows, basis), f32),
         in_specs=[any_space, any_space, any_space, pl.BlockSpec(memory_space=pltpu.SMEM)],
         out_specs=pl.BlockSpec(memory_space=pltpu.VMEM),
         scratch_shapes=[

time: 58.2 us -> 56.9 us (0.978)
  local copies, waits for them, and re-layouts: 1.28 us -> 0.6 us
  Pallas kernels: 56.7 us -> 56.1 us
    unnamed x1, local copies, waits for them, and re-layouts: 1.28 us -> 0.6 us
    pallas_call x1, Pallas kernels: 56.7 us -> 56.1 us  [on_device(): pl.pallas_call(kernel, out_shape=pltpu.VMEM((rows, basis), f32), in_specs...]
where the time goes in v4:
time: 56.9 us; the launch traced here: 56.8 us
  Pallas kernels  56.1 us (99%)
  local copies, waits for them, and re-layouts  0.6 us (1%)
    pallas_call x1, Pallas kernels, on_device(): pl.pallas_call(kernel, out_shape=pltpu.VMEM((rows, basis), f32), in_specs...  56.1 us

profile of v4, /device:TPU:1, one launch (start us, length us, event | category | flops | bytes accessed | tf_op | source)
XLA Modules:
  0.0 56.8 jit_solution(16640004032335383855)
XLA Ops:
  0.0 56.1 %shard_map.46 = f32[4,256]{1,0:T(4,128)S(1)} custom-call(bf16[256,4,256]{2,1,0:T(4,128)(2,1)} %ints.1, bf16[256,4,256]{2,1,0:T(4,128)(2,1)} %fit.1, bf16[4,1024]{1,0:T(4,128)(2,1)} %occ.1, s32[8,8]{1,0:T(8,128)} %pat.1), custom_call_target="tpu_custom_call" | custom-call | tf_op jit(solution)/shard_map/pallas_call | solution.py:253
  56.2 0.6 %copy.6 = f32[4,256]{1,0:T(4,128)} copy(f32[4,256]{1,0:T(4,128)S(1)} %shard_map.46) | data formatting | bytes 8192

commit v5 on v4

--- a/solution.py
+++ b/solution.py
@@ -190,22 +190,27 @@
 
     for core in range(NC):
         s_all[core] = s[:, core]
-    swap = pltpu.make_async_remote_copy(
-        src_ref=s_all.at[1 - c], dst_ref=r_x, send_sem=sendx_sem, recv_sem=x_sem,
-        device_id={"wide": wide_id(y, z, 1 - c), "narrow": n})
-    swap.start()
-    swap.wait_recv()
-    s_a[...] = (s_all[c] + r_x[...]).reshape(NY, NZ, rows, basis)
-
-    def copy_a(dy):
-        yy = lax.rem(y + dy, NY)
-        return pltpu.make_async_remote_copy(
-            src_ref=s_a.at[yy], dst_ref=r_a.at[y], send_sem=senda_sem, recv_sem=a_sem,
-            device_id={"wide": wide_id(yy, z, c), "narrow": n})
-
-    for dy in Y_ORDER:
-        if dy:
-            copy_a(dy).start()
+    half = NY // 2 * NZ
+
+    def swap(g):
+        part = pl.ds(g * half, half)
+        return pltpu.make_async_remote_copy(
+            src_ref=s_all.at[1 - c, part], dst_ref=r_x.at[part], send_sem=sendx_sem.at[g], recv_sem=x_sem.at[g],
+            device_id={"wide": wide_id(y, z, 1 - c), "narrow": n})
+
+    swap(0).start()
+    swap(1).start()
+
+    for g in range(2):
+        part = pl.ds(g * half, half)
+        swap(g).wait_recv()
+        s_a[pl.ds(g * (NY // 2), NY // 2)] = (s_all[c, part] + r_x[part]).reshape(NY // 2, NZ, rows, basis)
+        for yy in range(g * (NY // 2), (g + 1) * (NY // 2)):
+            @pl.when(y != yy)
+            def _():
+                pltpu.make_async_remote_copy(
+                    src_ref=s_a.at[yy], dst_ref=r_a.at[y], send_sem=senda_sem, recv_sem=a_sem,
+                    device_id={"wide": wide_id(yy, z, c), "narrow": n}).start()
     pltpu.make_async_copy(s_a.at[y], r_a.at[y], a_sem).start()
     pltpu.make_async_copy(r_a, r_a, a_sem).wait()
     s_b[...] = jnp.sum(r_a[...], axis=0)
@@ -234,7 +239,8 @@
     pltpu.make_async_copy(own, own, send2_sem).wait()
     rest = c_all.at[pl.ds(0, NX * NC - 1)]
     pltpu.make_async_copy(rest, rest, send2_sem).wait()
-    swap.wait_send()
+    swap(0).wait_send()
+    swap(1).wait_send()
     ra = r_a.at[pl.ds(0, NY - 1)]
     pltpu.make_async_copy(ra, ra, senda_sem).wait()
     rb = r_b.at[pl.ds(0, NH * NX * NZ - 1)]
@@ -269,7 +275,7 @@
             pltpu.VMEM((NY, NZ, rows, basis), f32),
             pltpu.VMEM((NZ, rows, basis), f32),
             pltpu.VMEM((NH * NX * NZ, rows, basis), f32),
-        ] + [dma] * 3 + [pltpu.SemaphoreType.DMA((NY,))] + [dma] * 8 + [
+        ] + [dma] * 3 + [dma((NY,)), dma] + [dma((2,))] + [dma] * 3 + [dma((2,))] + [dma] * 2 + [
             pltpu.SemaphoreType.REGULAR((4 * max(1, NY // 2 + NZ - 2),)), pltpu.SemaphoreType.REGULAR((4,))],
         compiler_params=pltpu.CompilerParams(collective_id=0, has_side_effects=True),
     )(integrals, fitted, occupied, pattern)

time: 56.9 us -> 56.8 us (level)
  the two profiles are of different devices: /device:TPU:1 before, /device:TPU:16 now
where the time goes in v5:
time: 56.8 us; the launch traced here: 56.6 us
  Pallas kernels  56 us (99%)
  local copies, waits for them, and re-layouts  0.6 us (1%)
    pallas_call x1, Pallas kernels, on_device(): pl.pallas_call(kernel, out_shape=pltpu.VMEM((rows, basis), f32), in_specs...  56 us

profile of v5, /device:TPU:16, one launch (start us, length us, event | category | flops | bytes accessed | tf_op | source)
XLA Modules:
  0.0 56.6 jit_solution(14957717959392916599)
XLA Ops:
  0.0 56.0 %shard_map.46 = f32[4,256]{1,0:T(4,128)S(1)} custom-call(bf16[256,4,256]{2,1,0:T(4,128)(2,1)} %ints.1, bf16[256,4,256]{2,1,0:T(4,128)(2,1)} %fit.1, bf16[4,1024]{1,0:T(4,128)(2,1)} %occ.1, s32[8,8]{1,0:T(8,128)} %pat.1), custom_call_target="tpu_custom_call" | custom-call | tf_op jit(solution)/shard_map/pallas_call | solution.py:259
  56.0 0.6 %copy.6 = f32[4,256]{1,0:T(4,128)} copy(f32[4,256]{1,0:T(4,128)S(1)} %shard_map.46) | data formatting | bytes 8192

commit v6 on v5

--- a/solution.py
+++ b/solution.py
@@ -83,14 +83,6 @@
     @pl.when(edge)
     def _():
         pl.semaphore_signal(barrier, inc=1, device_id=over)
-
-    lane = lax.broadcasted_iota(jnp.int32, (1, basis), 1) // (basis // NBLK)
-    for a in range(NBLK):
-        v = jnp.zeros((1, basis), jnp.float32)
-        for b in range(NBLK):
-            v = jnp.where(lane == b, pat[a, b].astype(jnp.float32), v)
-        mask[pl.ds(a * (basis // NBLK), basis // NBLK), :] = jnp.broadcast_to(
-            v, (basis // NBLK, basis)).astype(jnp.bfloat16)
 
     inner = (z < NZ - 1).astype(jnp.int32) + (z > 0).astype(jnp.int32)
     pl.semaphore_wait(barrier, 1 + NC * (2 + inner) + 2 + edge.astype(jnp.int32))
@@ -168,6 +160,14 @@
     @pl.when(jnp.logical_not(edge))
     def _():
         pl.semaphore_wait(cross.at[3], 1)
+
+    lane = lax.broadcasted_iota(jnp.int32, (1, basis), 1) // (basis // NBLK)
+    for a in range(NBLK):
+        v = jnp.zeros((1, basis), jnp.float32)
+        for b in range(NBLK):
+            v = jnp.where(lane == b, pat[a, b].astype(jnp.float32), v)
+        mask[pl.ds(a * (basis // NBLK), basis // NBLK), :] = jnp.broadcast_to(
+            v, (basis // NBLK, basis)).astype(jnp.bfloat16)
 
     pltpu.make_async_copy(c_all, c_all, all_sem).wait()
     panel = jnp.concatenate([c_all[k].reshape(basis, lanes) for k in range(NX * NC)], axis=1)

time: 56.8 us -> 56.7 us (level)
  no operation moved by 1% of the time
where the time goes in v6:
time: 56.7 us; the launch traced here: 56.5 us
  Pallas kernels  55.9 us (99%)
  local copies, waits for them, and re-layouts  0.6 us (1%)
    pallas_call x1, Pallas kernels, on_device(): pl.pallas_call(kernel, out_shape=pltpu.VMEM((rows, basis), f32), in_specs...  55.9 us

profile of v6, /device:TPU:16, one launch (start us, length us, event | category | flops | bytes accessed | tf_op | source)
XLA Modules:
  0.0 56.5 jit_solution(5164236419709195550)
XLA Ops:
  0.0 55.9 %shard_map.46 = f32[4,256]{1,0:T(4,128)S(1)} custom-call(bf16[256,4,256]{2,1,0:T(4,128)(2,1)} %ints.1, bf16[256,4,256]{2,1,0:T(4,128)(2,1)} %fit.1, bf16[4,1024]{1,0:T(4,128)(2,1)} %occ.1, s32[8,8]{1,0:T(8,128)} %pat.1), custom_call_target="tpu_custom_call" | custom-call | tf_op jit(solution)/shard_map/pallas_call | solution.py:259
  55.9 0.6 %copy.6 = f32[4,256]{1,0:T(4,128)} copy(f32[4,256]{1,0:T(4,128)S(1)} %shard_map.46) | data formatting | bytes 8192
